TPU v7x, 32 devices: a whole 2x2x4 slice. The times are simulated.
32 devices in a mesh: groups: 2 (over x), tm: 16 (over z, y, core).
Axes of the slice: x: 2, y: 2, z: 4, core: 2. Of those that a mesh axis runs over, the one named last changes fastest.
Arguments:
- loglik: float32 [4, 1024, 512], P('groups', None, 'tm'), parts along dimension 0, may hold values from -105 to 105
- trans_weight: float32 [256, 256], replicated, may hold values from 0 to 1, as said below
- block_mask: int32 [4, 4], replicated, may hold values from 0 to 1, as said below
- init_weight: float32 [256], replicated, may hold values from 0.01 to 1
- lengths: int32 [4], P('groups'), parts along dimension 0, may hold values from 512 to 1024, as said below
- pdf_map: int32 [256], replicated, may hold values from 0 to 511
Outputs:
- log_forward: float32 [4, 1024, 256], P('groups', 'tm'), parts along dimension 0
- log_gain: float32 [4, 1024], P('groups', 'tm'), parts along dimension 0
There are 2 independent parts, one for each index of `groups`. A program takes and returns all parts, laid end to end along the dimension named above; an argument that names none is the same for every part. Nothing has to cross between parts.
Inputs may be any that keep to these rules, and one draw needn't show every extreme that they name: `block_mask`: the diagonal blocks are always allowed. `lengths`: some utterance has all 1024 frames. `trans_weight`: every entry is positive.
All inputs are finite; a program needn't handle non-finite values.
Results may differ from a plain program's by a relative error of at most 0.0003.
Values sent between devices are 32-bit elements; how exact they have to be, the bound alone decides.
No kernel may reach another device: no remote copies, remote signals or barrier semaphores. Data moves between devices by JAX's collectives and lax.ppermute only.
A program may use at most 128 MiB of HBM per device.

v0:
```python
import jax
import jax.numpy as jnp
from jax import lax
from jax.sharding import PartitionSpec as P


def carried_in(part, axis, combine, identity):
    place = lax.axis_index(axis)
    gathered = lax.all_gather(part, axis)
    state = jnp.zeros_like(part) + jnp.asarray(identity, part.dtype)

    def one(turn, state):
        return combine(state, lax.dynamic_index_in_dim(gathered, turn, 0, False))

    return lax.fori_loop(0, place, one, state)


def transitions(trans_weight, block_mask):
    width = trans_weight.shape[0] // block_mask.shape[0]
    expanded = jnp.repeat(jnp.repeat(block_mask, width, axis=0), width, axis=1).astype(jnp.float32)
    masked = trans_weight * expanded
    return masked / jnp.sum(masked, axis=1, keepdims=True)


def rescale(matrix):
    return matrix / jnp.max(matrix, axis=(1, 2), keepdims=True)


def chain_product(earlier, later):
    joined = jnp.einsum("uij,ujk->uik", earlier, later, precision=lax.Precision.HIGHEST)
    return rescale(joined)


def shards(loglik, trans_weight, block_mask, init_weight, lengths, pdf_map):
    trans = transitions(trans_weight, block_mask)
    states = trans.shape[0]
    utts = loglik.shape[0]
    start = init_weight / jnp.sum(init_weight)
    g_vals = jnp.take(
        lax.all_to_all(loglik, "tm", split_axis=1, concat_axis=2, tiled=True), pdf_map, axis=2
    )
    top = jnp.max(g_vals, axis=2, keepdims=True)
    factors = jnp.exp(g_vals - top)
    tops = top[..., 0]
    frame_count = factors.shape[1]
    offset = lax.axis_index("tm") * frame_count
    frame_ids = offset + jnp.arange(frame_count, dtype=jnp.int32)
    live = frame_ids[None, :] < lengths[:, None]
    seq_factors = jnp.moveaxis(factors, 1, 0)
    seq_tops = jnp.moveaxis(tops, 1, 0)
    seq_live = jnp.moveaxis(live, 1, 0)
    identity = jnp.broadcast_to(jnp.eye(states, dtype=jnp.float32), (utts, states, states))

    def extend(index, matrices):
        factor = lax.dynamic_index_in_dim(factors, index, 1, keepdims=False)
        alive = lax.dynamic_index_in_dim(live, index, 1, keepdims=False)
        step_op = jnp.where(alive[:, None, None], trans[None, :, :] * factor[:, None, :], identity)
        return chain_product(matrices, step_op)

    local_op = lax.fori_loop(0, frame_count, extend, identity)
    earlier_op = carried_in(local_op, "tm", chain_product, identity)
    incoming = jnp.einsum("i,uik->uk", start, earlier_op, precision=lax.Precision.HIGHEST)
    incoming = incoming / jnp.sum(incoming, axis=1, keepdims=True)

    def advance(alpha, inputs):
        factor, top, alive = inputs
        v_new = jnp.dot(alpha, trans, precision=lax.Precision.HIGHEST) * factor
        total = jnp.sum(v_new, axis=1, keepdims=True)
        fresh = jnp.where(alive[:, None], v_new / total, alpha)
        gain = jnp.where(alive, jnp.log(total[:, 0]) + top, jnp.float32(0.0))
        return (fresh, (fresh, gain))

    _, (occupied, gains) = lax.scan(advance, incoming, (seq_factors, seq_tops, seq_live))
    return (jnp.log(jnp.moveaxis(occupied, 0, 1)), jnp.moveaxis(gains, 0, 1))


def solution(mesh):
    return jax.shard_map(
        shards,
        mesh=mesh,
        in_specs=(P("groups", None, "tm"), P(), P(), P(), P("groups"), P()),
        out_specs=(P("groups", "tm", None), P("groups", "tm")),
        check_vma=False,
    )
```

profile of v0, /device:TPU:29, one launch (start us, length us, event | category | flops | bytes accessed | tf_op | source)
XLA Modules:
  0.0 243.3 jit_solution(11408980057508970936)
XLA Ops:
  7.2 1.4 copy.32
  8.6 1.7 reshape.49
  10.3 6.3 %all-to-all-start = ((f32[16,1,4096]{2,1,0:T(1,128)}), f32[16,1,4096]{2,1,0:T(1,128)S(1)}, u32[]{:S(2)}, u32[]{:S(2)}) async-start(f32[16,1,4096]{2,1,0:T(1,128)} %reshape.49), calls=%async_computation | async-start | bytes 524288 | tf_op jit(solution)/shard_map/all_to_all | solution.py:40
  17.4 1.1 copy.31
  21.0 2.7 %all-to-all-done = f32[16,1,4096]{2,1,0:T(1,128)S(1)} async-done(((f32[16,1,4096]{2,1,0:T(1,128)}), f32[16,1,4096]{2,1,0:T(1,128)S(1)}, u32[]{:S(2)}, u32[]{:S(2)}) %all-to-all-start) | async-done | bytes 262176 | tf_op jit(solution)/shard_map/all_to_all | solution.py:40
  24.2 1.3 reduce.2
  25.5 0.9 reshape.50
  27.3 1.0 gather_fusion
  29.2 61.0 %while.40 = (s32[]{:T(128)}, f32[2,256,256]{1,2,0:T(8,128)S(1)}, pred[2,64]{0,1:T(8,128)(4,1)S(1)}, f32[256,256]{0,1:T(8,128)S(1)}, f32[2,64,256]{2,0,1:T(2,128)S(1)}, /*index=5*/f32[256,256]{0,1:T(8,128)S(1)}, s32[]{:T(128)}) while((s32[]{:T(128)}, f32[2,256,256]{1,2,0:T(8,128)S(1)}, pred[2,64]{0,1:T(8,128)(4,1)S(1)}, ...), condition=%wide.region_5.6_spmd.clone, body=%wide.region_3.5_spmd.clone.sunk | while | flops 403177472 | bytes 2627691 | solution.py:60
  36.9 0.8 fusion.48
  41.6 0.8 fusion.48
  45.5 0.8 fusion.48
  46.4 0.8 fusion.48
  90.2 1.0 copy.36
  93.4 71.4 %all-gather.3.cloned.1.call-done = f32[32,256,256]{2,1,0:T(8,128)} async-done(((f32[2,256,256]{2,1,0:T(8,128)}), f32[32,256,256]{2,1,0:T(8,128)}) %all-gather.3.cloned.1.call-update) | async-done | bytes 8388624 | tf_op jit(solution)/shard_map/all_gather | solution.py:9
  164.8 34.2 %while.38 = (s32[]{:T(128)}, f32[2,256,256]{1,2,0:T(8,128)S(1)}, s32[]{:T(128)}, f32[16,2,256,256]{3,2,1,0:T(8,128)}, s32[]{:T(128)}, /*index=5*/s32[]{:T(128)}, s32[]{:T(128)}) while((s32[]{:T(128)}, f32[2,256,256]{1,2,0:T(8,128)S(1)}, s32[]{:T(128)}, f32[16,2,256,256]{3,2,1,0:T(8,128)}, s32[]{:T(128)}, /*index=5*/s32[]{:T(128)}, ...), condition=%wide.region_8.9_spmd, body=%wide.region_6.8_spmd.sunk | while | flops 402915328 | bytes 2621571 | solution.py:15
  164.8 2.1 fusion.41
  167.1 2.1 fusion.41
  169.4 2.1 fusion.41
  171.7 2.1 fusion.41
  173.9 2.1 fusion.41
  176.2 2.1 fusion.41
  178.5 2.1 fusion.41
  180.8 2.1 fusion.41
  183.1 2.1 fusion.41
  185.3 2.1 fusion.41
  187.6 2.1 fusion.41
  189.9 2.1 fusion.41
  192.2 2.1 fusion.41
  194.5 2.1 fusion.41
  196.8 2.1 fusion.41
  199.7 35.4 %while.39 = (s32[]{:T(128)}, f32[2,256]{1,0:T(2,128)S(1)}, f32[64,2,256]{2,0,1:T(8,128)S(1)}, f32[64,2]{1,0:T(8,128)S(1)}, pred[64,2]{1,0:T(8,128)(4,1)S(1)}, /*...) while((s32[]{:T(128)}, f32[2,256]{1,0:T(2,128)S(1)}, ...), condition=%wide.region_12.13_spmd, body=%wide.region_10.12_spmd.sunk | while | flops 1574916 | bytes 282809 | solution.py:73
  (755 shorter events, 99.8 us)
Async XLA Ops:
  10.3 13.4 %all-to-all-start = ((f32[16,1,4096]{2,1,0:T(1,128)}), f32[16,1,4096]{2,1,0:T(1,128)S(1)}, u32[]{:S(2)}, u32[]{:S(2)}) async-start(f32[16,1,4096]{2,1,0:T(1,128)} %reshape.49), calls=%async_computation | async-start | bytes 524288 | tf_op jit(solution)/shard_map/all_to_all | solution.py:40
  16.7 148.1 %all-gather.3.cloned.1.call-start = ((), (), s32[]{:S(2)}) async-start(), calls=%async_computation.1 | async-start | bytes 8912896 | tf_op jit(solution)/shard_map/all_gather | solution.py:9
  29.0 62.5 %copy-start = (f32[256]{0:T(256)S(1)}, f32[256]{0:T(256)}, u32[]{:S(2)}) copy-start(f32[256]{0:T(256)} %param.15) | copy-start | bytes 3076
  29.0 63.7 %copy-start.1 = (s32[2]{0:T(128)S(1)}, s32[2]{0:T(128)}, u32[]{:S(2)}) copy-start(s32[2]{0:T(128)} %param.16) | copy-start | bytes 28
Sparse Core Ops, SparseCore 0:
  91.4 73.2 all-gather.2
where the time goes:
time: 244 us; the launch traced here: 243 us
  matrix products  104 us (43%)
  waiting for transfers between devices  74.1 us (30%)
  other arithmetic  21.8 us (9%)
  local copies, waits for them, and re-layouts  17.6 us (7%)
  between operations  14.2 us (6%)
  starting transfers between devices  6.37 us (3%)
  loops' own time  5.33 us (2%)
    dot_general x79, matrix products, chain_product(): jnp.einsum('uij,ujk->uik', earlier, later, precision=lax.Precision.HIGHEST)  82 us
    all_gather x1, waiting for transfers between devices, carried_in(): gathered = lax.all_gather(part, axis)  71.4 us
    dot_general x64, matrix products, advance(): v_new = jnp.dot(alpha, trans, precision=lax.Precision.HIGHEST) * factor  21.3 us
    div x79, other arithmetic, rescale(): return matrix / jnp.max(matrix, axis=(1, 2), keepdims=True)  8.92 us
    all_to_all x1, starting transfers between devices, shards(): lax.all_to_all(loglik, 'tm', split_axis=1, concat_axis=2, tiled=True)  6.33 us
    unnamed x9, local copies, waits for them, and re-layouts  5.28 us
    select_n x64, other arithmetic, advance(): fresh = jnp.where(alive[:, None], v_new / total, alpha)  5.19 us
  transfers between devices with their start and end apart: 2, of which 2 were waited for; matrix products, arithmetic and copies ran while one was open for 3% of the time, Pallas kernels for 0%

commit v1 on v0

--- a/solution.py
+++ b/solution.py
@@ -36,9 +36,16 @@
     states = trans.shape[0]
     utts = loglik.shape[0]
     start = init_weight / jnp.sum(init_weight)
-    g_vals = jnp.take(
-        lax.all_to_all(loglik, "tm", split_axis=1, concat_axis=2, tiled=True), pdf_map, axis=2
-    )
+
+    def raise_limits(field_in, shard_axis):
+        return jnp.concatenate(
+            lax.all_to_all(
+                jnp.stack(jnp.split(field_in, lax.axis_size(shard_axis), axis=1)), shard_axis, 0, 0
+            ),
+            axis=2,
+        )
+
+    g_vals = jnp.take(raise_limits(loglik, "tm"), pdf_map, axis=2)
     top = jnp.max(g_vals, axis=2, keepdims=True)
     factors = jnp.exp(g_vals - top)
     tops = top[..., 0]

time: 244 us -> 255 us (1.045)
  local copies, waits for them, and re-layouts: 17.6 us -> 27.2 us
    unnamed x9 -> x23, local copies, waits for them, and re-layouts: 5.28 us -> 14.4 us
  transfers between devices with their start and end apart: 2 -> 2, of which waited for: 2 -> 2; matrix products, arithmetic and copies ran while one was open for 3% -> 2% of each run, Pallas kernels for 0% -> 0%
where the time goes in v1:
time: 255 us; the launch traced here: 253 us
  matrix products  104 us (41%)
  waiting for transfers between devices  74.1 us (29%)
  local copies, waits for them, and re-layouts  27.2 us (11%)
  other arithmetic  21.8 us (9%)
  between operations  14.2 us (6%)
  starting transfers between devices  6.37 us (2%)
  loops' own time  5.33 us (2%)
    dot_general x79, matrix products, chain_product(): jnp.einsum('uij,ujk->uik', earlier, later, precision=lax.Precision.HIGHEST)  82 us
    all_gather x1, waiting for transfers between devices, carried_in(): gathered = lax.all_gather(part, axis)  71.4 us
    dot_general x64, matrix products, advance(): v_new = jnp.dot(alpha, trans, precision=lax.Precision.HIGHEST) * factor  21.3 us
    unnamed x23, local copies, waits for them, and re-layouts  14.4 us
    div x79, other arithmetic, rescale(): return matrix / jnp.max(matrix, axis=(1, 2), keepdims=True)  8.92 us
    all_to_all x1, starting transfers between devices, raise_limits(): lax.all_to_all(jnp.stack(jnp.split(field_in, lax.axis_size(shard_axis), a...  6.33 us
    select_n x64, other arithmetic, advance(): fresh = jnp.where(alive[:, None], v_new / total, alpha)  5.19 us
  transfers between devices with their start and end apart: 2, of which 2 were waited for; matrix products, arithmetic and copies ran while one was open for 2% of the time, Pallas kernels for 0%

profile of v1, /device:TPU:29, one launch (start us, length us, event | category | flops | bytes accessed | tf_op | source)
XLA Modules:
  0.0 252.9 jit_solution(10340044332833420688)
XLA Ops:
  7.9 0.8 constant_dynamic-update-slice_fusion.14
  9.5 0.8 constant_dynamic-update-slice_fusion.12
  11.1 0.8 constant_dynamic-update-slice_fusion.10
  12.7 0.8 constant_dynamic-update-slice_fusion.8
  14.3 0.8 constant_dynamic-update-slice_fusion.6
  15.9 0.8 constant_dynamic-update-slice_fusion.4
  19.9 1.0 reshape.57
  21.0 6.3 %all-to-all-start = ((f32[16,1,4096]{2,1,0:T(1,128)}), f32[16,1,4096]{2,1,0:T(1,128)S(1)}, u32[]{:S(2)}, u32[]{:S(2)}) async-start(f32[16,1,4096]{2,1,0:T(1,128)} %reshape.57), calls=%async_computation | async-start | bytes 524288 | tf_op jit(solution)/shard_map/all_to_all | solution.py:42
  28.1 1.1 copy.31
  31.6 2.7 %all-to-all-done = f32[16,1,4096]{2,1,0:T(1,128)S(1)} async-done(((f32[16,1,4096]{2,1,0:T(1,128)}), f32[16,1,4096]{2,1,0:T(1,128)S(1)}, u32[]{:S(2)}, u32[]{:S(2)}) %all-to-all-start) | async-done | bytes 262176 | tf_op jit(solution)/shard_map/all_to_all | solution.py:42
  34.8 1.3 reduce.2
  36.8 1.0 gather_fusion
  38.7 61.0 %while.40 = (s32[]{:T(128)}, f32[2,256,256]{1,2,0:T(8,128)S(1)}, pred[2,64]{0,1:T(8,128)(4,1)S(1)}, f32[256,256]{0,1:T(8,128)S(1)}, f32[2,64,256]{2,0,1:T(2,128)S(1)}, /*index=5*/f32[256,256]{0,1:T(8,128)S(1)}, s32[]{:T(128)}) while((s32[]{:T(128)}, f32[2,256,256]{1,2,0:T(8,128)S(1)}, pred[2,64]{0,1:T(8,128)(4,1)S(1)}, ...), condition=%wide.region_5.6_spmd.clone, body=%wide.region_3.5_spmd.clone.sunk | while | flops 403177472 | bytes 2627691 | solution.py:67
  99.8 1.0 copy.35
  102.9 71.4 %all-gather.3.cloned.1.call-done = f32[32,256,256]{2,1,0:T(8,128)} async-done(((f32[2,256,256]{2,1,0:T(8,128)}), f32[32,256,256]{2,1,0:T(8,128)}) %all-gather.3.cloned.1.call-update) | async-done | bytes 8388624 | tf_op jit(solution)/shard_map/all_gather | solution.py:9
  174.3 34.2 %while.38 = (s32[]{:T(128)}, f32[2,256,256]{1,2,0:T(8,128)S(1)}, s32[]{:T(128)}, f32[16,2,256,256]{3,2,1,0:T(8,128)}, s32[]{:T(128)}, /*index=5*/s32[]{:T(128)}, s32[]{:T(128)}) while((s32[]{:T(128)}, f32[2,256,256]{1,2,0:T(8,128)S(1)}, s32[]{:T(128)}, f32[16,2,256,256]{3,2,1,0:T(8,128)}, s32[]{:T(128)}, /*index=5*/s32[]{:T(128)}, ...), condition=%wide.region_8.9_spmd, body=%wide.region_6.8_spmd.sunk | while | flops 402915328 | bytes 2621571 | solution.py:15
  174.4 2.1 fusion.41
  176.7 2.1 fusion.41
  178.9 2.1 fusion.41
  181.2 2.1 fusion.41
  183.5 2.1 fusion.41
  185.8 2.1 fusion.41
  188.1 2.1 fusion.41
  190.3 2.1 fusion.41
  192.6 2.1 fusion.41
  194.9 2.1 fusion.41
  197.2 2.1 fusion.41
  199.5 2.1 fusion.41
  201.7 2.1 fusion.41
  204.0 2.1 fusion.41
  206.3 2.1 fusion.41
  209.3 35.4 %while.39 = (s32[]{:T(128)}, f32[2,256]{1,0:T(2,128)S(1)}, f32[64,2,256]{2,0,1:T(8,128)S(1)}, f32[64,2]{1,0:T(8,128)S(1)}, pred[64,2]{1,0:T(8,128)(4,1)S(1)}, /*...) while((s32[]{:T(128)}, f32[2,256]{1,0:T(2,128)S(1)}, ...), condition=%wide.region_12.13_spmd, body=%wide.region_10.12_spmd.sunk | while | flops 1574916 | bytes 282809 | solution.py:80
  (771 shorter events, 110.6 us)
Async XLA Ops:
  21.0 13.4 %all-to-all-start = ((f32[16,1,4096]{2,1,0:T(1,128)}), f32[16,1,4096]{2,1,0:T(1,128)S(1)}, u32[]{:S(2)}, u32[]{:S(2)}) async-start(f32[16,1,4096]{2,1,0:T(1,128)} %reshape.57), calls=%async_computation | async-start | bytes 524288 | tf_op jit(solution)/shard_map/all_to_all | solution.py:42
  27.3 147.0 %all-gather.3.cloned.1.call-start = ((), (), s32[]{:S(2)}) async-start(), calls=%async_computation.1 | async-start | bytes 8912896 | tf_op jit(solution)/shard_map/all_gather | solution.py:9
  38.5 62.5 %copy-start = (f32[256]{0:T(256)S(1)}, f32[256]{0:T(256)}, u32[]{:S(2)}) copy-start(f32[256]{0:T(256)} %param.15) | copy-start | bytes 3076
  38.5 63.7 %copy-start.1 = (s32[2]{0:T(128)S(1)}, s32[2]{0:T(128)}, u32[]{:S(2)}) copy-start(s32[2]{0:T(128)} %param.16) | copy-start | bytes 28
Sparse Core Ops, SparseCore 0:
  101.0 73.2 all-gather.2
